TPU v7x, 512 devices: a whole 4x4x16 slice. The times are simulated.
512 devices in a mesh: dp: 8 (over z_hi, y), expert: 64 (over z_lo, x, core).
Axes of the slice: x: 4, y: 4, z: 16 (z_hi: 2, z_lo: 8; z = z_hi * 8 + z_lo), core: 2. Of those that a mesh axis runs over, the one named last changes fastest.
Arguments:
- hidden_rows: bfloat16 [768, 65536], P(None, ('dp', 'expert')), may hold values from -6 to 6
- grad_rows: bfloat16 [65536, 2560], P(('dp', 'expert')), may hold values from -0.1796875 to 0.1796875
- block_slot: int32 [512, 1], P(('dp', 'expert')), may hold values from 0 to 1
- live_rows: int32 [512], P(('dp', 'expert')), may hold values from 16 to 128
- replica_plan: int32 [64], replicated, may hold values from 0 to 15
- master: float32 [64, 768, 640], P('expert', 'dp'), may hold values from -0.21875 to 0.21875
- moment_one: float32 [64, 768, 640], P('expert', 'dp'), may hold values from -1.8 to 1.8
- moment_two: float32 [64, 768, 640], P('expert', 'dp'), may hold values from 0.01 to 1
Outputs:
- master_new: float32 [64, 768, 640], P('expert', 'dp')
- first_new: float32 [64, 768, 640], P('expert', 'dp')
- second_new: float32 [64, 768, 640], P('expert', 'dp')
- replica_weight: bfloat16 [64, 768, 2560], P('expert', 'dp')
Inputs may be any that keep to these rules, and one draw needn't show every extreme that they name: replica_plan[j] is the expert of which the devices at index j along the expert axis host a replica; it may equal j mod 16. `block_slot`: 0 marks a block of the primary expert, 1 a block of the replica.
All inputs are finite; a program needn't handle non-finite values.
Results may differ from a plain program's by a relative error of at most 0.001.
Values may be sent and summed in bfloat16 or wider, within the bound.
A program may use at most 64 MiB of HBM per device.

v0:
```python
import jax
import jax.numpy as jnp
from jax import lax
from jax.sharding import PartitionSpec as P

QUART = 4
beta_one = 0.9
beta_two = 0.95
learn_rate = 0.01
decay_rate = 0.1
epsilon = 1e-08
step_count = 10.0


def from_behind(block, axis, distance):
    devices = range(lax.axis_size(axis))
    route = [((i - distance) % len(devices), i) for i in devices]
    return lax.ppermute(block, axis, route)


def adam_update(weights, first, second, gradient):
    first_next = beta_one * first + (1.0 - beta_one) * gradient
    second_next = beta_two * second + (1.0 - beta_two) * gradient * gradient
    scaled_first = first_next / (1.0 - beta_one**step_count)
    scaled_second = second_next / (1.0 - beta_two**step_count)
    direction = scaled_first / (jnp.sqrt(scaled_second) + epsilon)
    weights_next = weights - learn_rate * (direction + decay_rate * weights)
    return (weights_next, first_next, second_next)


def per_device(
    hidden_rows, grad_rows, block_slot, live_rows, replica_plan, master, moment_one, moment_two
):
    expert_count = lax.axis_size("expert")
    group_count = lax.axis_size("dp")
    own_index = lax.axis_index("expert")
    group_index = lax.axis_index("dp")
    hidden_units, tok_rows = hidden_rows.shape
    model_width = grad_rows.shape[1]
    block_count = block_slot.shape[1]
    block_span = tok_rows // block_count
    owner_count = expert_count // QUART
    block_width = model_width // QUART
    share_rows = hidden_units // group_count
    own_block = own_index // owner_count
    kept_rows = lax.iota(jnp.int32, tok_rows) < live_rows[0]
    row_slot = jnp.repeat(block_slot[0], block_span)
    zero_rows = jnp.zeros_like(grad_rows)
    grad_primary = jnp.where((kept_rows & (row_slot == 0))[:, None], grad_rows, zero_rows)
    grad_replica = jnp.where((kept_rows & (row_slot == 1))[:, None], grad_rows, zero_rows)
    replica_terms = jnp.dot(hidden_rows, grad_replica, preferred_element_type=jnp.float32).astype(
        jnp.bfloat16
    )
    primary_part = jnp.dot(hidden_rows, grad_primary, preferred_element_type=jnp.float32).reshape(
        hidden_units, QUART, block_width
    )
    primary_owned = lax.dynamic_index_in_dim(primary_part, own_block, 1, False)
    for step in range(1, QUART):
        target = (own_block + step) % QUART
        piece = lax.dynamic_index_in_dim(primary_part, target, 1, False)
        primary_owned = primary_owned + from_behind(piece, "expert", step * owner_count)
    expert_ids = lax.iota(jnp.int32, owner_count)
    holders = (replica_plan[None, :] == expert_ids[:, None]).astype(jnp.bfloat16)
    sectioned = replica_terms.reshape(
        expert_count, hidden_units // expert_count, QUART, block_width
    )
    pieces = lax.all_to_all(sectioned, "expert", split_axis=0, concat_axis=0, tiled=True)
    summed = jnp.einsum("es,skqd->qekd", holders, pieces, preferred_element_type=jnp.float32)
    summed = summed.reshape(expert_count, pieces.shape[1], pieces.shape[3])
    owned = lax.all_to_all(summed, "expert", split_axis=0, concat_axis=0, tiled=True).reshape(
        hidden_units, block_width
    )
    group_part = primary_owned + owned
    group_total = lax.psum(group_part, "dp")
    gradient = lax.dynamic_slice_in_dim(group_total, group_index * share_rows, share_rows, 0)
    weights_next, first_next, second_next = adam_update(
        master[0], moment_one[0], moment_two[0], gradient
    )
    fresh = weights_next.astype(jnp.bfloat16)
    chooser = (replica_plan[:, None] == expert_ids[None, :]).astype(jnp.bfloat16)
    sectioned_fresh = fresh.reshape(expert_count, 1, share_rows * block_width // expert_count)
    pieces = lax.all_to_all(sectioned_fresh, "expert", split_axis=0, concat_axis=0, tiled=True)
    grouped = pieces.reshape(QUART, owner_count, pieces.shape[1], pieces.shape[2])
    chosen = jnp.einsum(
        "je,qekc->jkqc", chooser, grouped, preferred_element_type=jnp.float32
    ).astype(jnp.bfloat16)
    received = lax.all_to_all(chosen, "expert", split_axis=0, concat_axis=0, tiled=True)
    blocks = jnp.transpose(received[:, 0], (1, 0, 2)).reshape(QUART, share_rows, block_width)
    replica_weight = jnp.transpose(blocks, (1, 0, 2)).reshape(share_rows, model_width)
    return (weights_next[None], first_next[None], second_next[None], replica_weight[None])


def solution(mesh):
    return jax.shard_map(
        per_device,
        mesh=mesh,
        in_specs=(
            P(None, ("dp", "expert")),
            P(("dp", "expert"), None),
            P(("dp", "expert"), None),
            P(("dp", "expert")),
            P(),
            P("expert", "dp", None),
            P("expert", "dp", None),
            P("expert", "dp", None),
        ),
        out_specs=(
            P("expert", "dp", None),
            P("expert", "dp", None),
            P("expert", "dp", None),
            P("expert", "dp", None),
        ),
        check_vma=False,
    )
```

profile of v0, /device:TPU:25, one launch (start us, length us, event | category | flops | bytes accessed | tf_op | source)
XLA Modules:
  0.0 986.9 jit_solution(8224352198364253314)
XLA Ops:
  7.2 0.0 copy-start
  8.5 0.0 copy-done
  8.5 4.3 fusion
  12.8 6.4 copy.50
  19.2 7.6 reshape.58
  26.8 0.0 copy-start.5
  26.8 190.7 %all_to_all.20 = bf16[64,12,4,640]{3,2,1,0:T(4,128)(2,1)S(1)} all-to-all(bf16[64,12,4,640]{3,2,1,0:T(4,128)(2,1)} %reshape.58), channel_id=1, replica_groups=mesh['dp'=8,'expert'=64] {'expert'}, dimensions={0} | all-to-all | bytes 7864320 | tf_op jit(solution)/shard_map/all_to_all | solution.py:67
  217.5 0.0 copy-done.5
  217.5 0.7 fusion.1
  218.1 2.7 copy.52
  220.8 0.0 copy-start.1
  220.8 8.7 all-to-all-start.1
  229.5 0.0 all-reduce.2.cloned.1.call-start
  229.6 0.0 copy-done.1
  229.6 1.3 fusion.8
  230.9 3.2 constant_dynamic-slice_fusion.3
  234.2 2.9 copy.47
  237.1 4.2 collective-permute-start
  241.2 2.9 copy.48
  244.1 7.2 collective-permute-start.1
  251.3 2.9 copy.49
  254.2 5.1 collective-permute-start.2
  259.2 2.9 copy.46
  262.1 276.0 %all-to-all-done.1 = f32[64,12,640]{2,1,0:T(8,128)S(1)} async-done(((f32[64,12,640]{2,1,0:T(8,128)}), f32[64,12,640]{2,1,0:T(8,128)S(1)}, u32[]{:S(2)}, u32[]{:S(2)}) %all-to-all-start.1) | async-done | bytes 1966112 | tf_op jit(solution)/shard_map/all_to_all | solution.py:70
  538.1 1.4 reshape.60
  539.5 0.0 collective-permute-done
  539.5 103.2 %collective-permute-done.1 = f32[768,640]{1,0:T(8,128)} collective-permute-done((f32[768,640]{1,0:T(8,128)}, f32[768,640]{1,0:T(8,128)}, u32[]{:S(2)}, u32[]{:S(2)}) %collective-permute-start.1) | collective-permute-done | bytes 1966112 | tf_op jit(solution)/shard_map/ppermute | solution.py:18
  642.8 0.0 collective-permute-done.2
  642.8 5.6 fusion.5
  648.4 0.0 copy-start.2
  648.4 0.0 copy-start.3
  648.4 0.0 copy-start.4
  648.4 0.0 all-reduce.2.cloned.1.call-update
  648.4 264.2 %all-reduce.2.cloned.1.call-done = f32[768,640]{1,0:T(8,128)} async-done(((f32[768,640]{1,0:T(8,128)}), f32[768,640]{1,0:T(8,128)}) %all-reduce.2.cloned.1.call-update) | async-done | bytes 1966096 | tf_op jit(solution)/shard_map/psum | solution.py:74
  912.6 0.0 copy-done.2
  912.6 0.0 copy-done.3
  912.6 0.0 copy-done.4
  912.6 1.9 fusion.27
  914.5 0.2 reshape.66
  914.7 0.5 broadcast.46
  915.2 1.4 reduce
  916.7 0.2 reshape.68
  916.8 24.4 %all_to_all.21 = bf16[64,2,480]{2,1,0:T(2,128)(2,1)S(1)} all-to-all(bf16[64,2,480]{2,1,0:T(2,128)(2,1)S(1)} %reshape.68), channel_id=1, replica_groups=mesh['dp'=8,'expert'=64] {'expert'}, dimensions={0} | all-to-all | bytes 245760 | tf_op jit(solution)/shard_map/all_to_all | solution.py:82
  941.2 0.2 reshape.69
  941.5 0.3 fusion.6
  941.8 0.4 copy.54
  942.2 35.7 %all_to_all.22 = bf16[64,1,4,960]{3,2,1,0:T(4,128)(2,1)S(1)} all-to-all(bf16[64,1,4,960]{3,2,1,0:T(4,128)(2,1)S(1)} %copy.54), channel_id=1, replica_groups=mesh['dp'=8,'expert'=64] {'expert'}, dimensions={0} | all-to-all | bytes 983040 | tf_op jit(solution)/shard_map/all_to_all | solution.py:87
  977.9 0.2 copy.55
  978.1 0.8 reshape.63
  978.9 0.3 copy.56
  979.1 1.0 broadcast_in_dim_reshape.3
  (2 shorter events, 0.1 us)
Async XLA Ops:
  7.2 1.4 copy-start
  26.8 190.7 %copy-start.5 = (s32[64]{0:T(128)S(1)}, s32[64]{0:T(128)}, u32[]{:S(2)}) copy-start(s32[64]{0:T(128)} %param.12) | copy-start | bytes 772
  220.8 8.8 copy-start.1
  220.8 317.3 %all-to-all-start.1 = ((f32[64,12,640]{2,1,0:T(8,128)}), f32[64,12,640]{2,1,0:T(8,128)S(1)}, u32[]{:S(2)}, u32[]{:S(2)}) async-start(f32[64,12,640]{2,1,0:T(8,128)} %copy.52), calls=%async_computation.1 | async-start | bytes 5242880 | tf_op jit(solution)/shard_map/all_to_all | solution.py:70
  229.5 683.1 %all-reduce.2.cloned.1.call-start = ((), (), s32[]{:S(2)}) async-start(), calls=%async_computation.4 | async-start | bytes 3932160 | tf_op jit(solution)/shard_map/psum | solution.py:74
  237.1 302.5 %collective-permute-start = (f32[768,640]{1,0:T(8,128)}, f32[768,640]{1,0:T(8,128)}, u32[]{:S(2)}, u32[]{:S(2)}) collective-permute-start(f32[768,640]{1,0:T(8,128)} %bitcast.75), channel_id=1, source_target_pairs={{48,0},{49,1},{50,2},{51,3},{52,4},{53,5},{54,6},{55,7},{56,8},{57... | collective-permute-start | bytes 5898248 | tf_op jit(solution)/shard_map/ppermute | solution.py:18
  244.1 398.7 %collective-permute-start.1 = (f32[768,640]{1,0:T(8,128)}, f32[768,640]{1,0:T(8,128)}, u32[]{:S(2)}, u32[]{:S(2)}) collective-permute-start(f32[768,640]{1,0:T(8,128)} %bitcast.76), channel_id=1, source_target_pairs={{32,0},{33,1},{34,2},{35,3},{36,4},{37,5},{38,6},{39,7},{40,8},{41... | collective-permute-start | bytes 5898248 | tf_op jit(solution)/shard_map/ppermute | solution.py:18
  254.2 388.6 %collective-permute-start.2 = (f32[768,640]{1,0:T(8,128)}, f32[768,640]{1,0:T(8,128)}, u32[]{:S(2)}, u32[]{:S(2)}) collective-permute-start(f32[768,640]{1,0:T(8,128)} %bitcast.77), channel_id=1, source_target_pairs={{16,0},{17,1},{18,2},{19,3},{20,4},{21,5},{22,6},{23,7},{24,8},{25... | collective-permute-start | bytes 5898248 | tf_op jit(solution)/shard_map/ppermute | solution.py:18
  648.4 264.2 %copy-start.2 = (f32[1,96,640]{2,1,0:T(8,128)S(1)}, f32[1,96,640]{2,1,0:T(8,128)}, u32[]{:S(2)}) copy-start(f32[1,96,640]{2,1,0:T(8,128)} %param.15) | copy-start | bytes 737284
  648.4 264.2 %copy-start.3 = (f32[1,96,640]{2,1,0:T(8,128)S(1)}, f32[1,96,640]{2,1,0:T(8,128)}, u32[]{:S(2)}) copy-start(f32[1,96,640]{2,1,0:T(8,128)} %param.14) | copy-start | bytes 737284
  648.4 264.2 %copy-start.4 = (f32[1,96,640]{2,1,0:T(8,128)S(1)}, f32[1,96,640]{2,1,0:T(8,128)}, u32[]{:S(2)}) copy-start(f32[1,96,640]{2,1,0:T(8,128)} %param.13) | copy-start | bytes 737284
Sparse Core Ops, SparseCore 0:
  648.5 264.0 all-reduce.1
where the time goes:
time: 988 us; the launch traced here: 987 us
  waiting for transfers between devices  643 us (65%)
  blocking collectives  251 us (25%)
  local copies, waits for them, and re-layouts  36.5 us (4%)
  starting transfers between devices  25.1 us (3%)
  between operations  15.6 us (2%)
    all_to_all x1, waiting for transfers between devices, per_device(): lax.all_to_all(summed, 'expert', split_axis=0, concat_axis=0, tiled=True)  276 us
    psum x1, waiting for transfers between devices, per_device(): group_total = lax.psum(group_part, 'dp')  264 us
    all_to_all x1, blocking collectives, per_device(): lax.all_to_all(sectioned, 'expert', split_axis=0, concat_axis=0, tiled=True)  191 us
    ppermute x3, waiting for transfers between devices, from_behind(): return lax.ppermute(block, axis, route)  103 us
    all_to_all x1, blocking collectives, per_device(): lax.all_to_all(chosen, 'expert', split_axis=0, concat_axis=0, tiled=True)  35.7 us
    all_to_all x1, blocking collectives, per_device(): lax.all_to_all(sectioned_fresh, 'expert', split_axis=0, concat_axis=0, ti...  24.4 us
  transfers between devices with their start and end apart: 5, of which 3 were waited for; matrix products, arithmetic and copies ran while one was open for 2% of the time, Pallas kernels for 0%

commit v1 on v0

--- a/solution.py
+++ b/solution.py
@@ -71,7 +71,7 @@
         hidden_units, block_width
     )
     group_part = primary_owned + owned
-    group_total = lax.psum(group_part, "dp")
+    group_total = jnp.sum(lax.all_gather(group_part, "dp"), axis=0)
     gradient = lax.dynamic_slice_in_dim(group_total, group_index * share_rows, share_rows, 0)
     weights_next, first_next, second_next = adam_update(
         master[0], moment_one[0], moment_two[0], gradient

time: 988 us -> 1280 us (1.30)
  waiting for transfers between devices: 643 us -> 908 us
  blocking collectives: 251 us -> 272 us
    all_gather x0 -> x1, waiting for transfers between devices: none -> 529 us  [per_device(): group_total = jnp.sum(lax.all_gather(group_part, 'dp'), axis=0)]
    psum x1 -> x0, waiting for transfers between devices: 264 us -> none  [per_device(): group_total = lax.psum(group_part, 'dp')]
    all_to_all x1, blocking collectives: 24.4 us -> 45.4 us  [per_device(): lax.all_to_all(sectioned_fresh, 'expert', split_axis=0, concat_axis=0, ti...]
  transfers between devices with their start and end apart: 5 -> 5, of which waited for: 3 -> 3; matrix products, arithmetic and copies ran while one was open for 2% -> 1% of each run, Pallas kernels for 0% -> 0%
where the time goes in v1:
time: 1280 us
  waiting for transfers between devices  908 us (71%)
  blocking collectives  272 us (21%)
  local copies, waits for them, and re-layouts  36.4 us (3%)
  starting transfers between devices  25.3 us (2%)
  between operations  15.6 us (1%)
  other arithmetic  14.6 us (1%)
    all_gather x1, waiting for transfers between devices, per_device(): group_total = jnp.sum(lax.all_gather(group_part, 'dp'), axis=0)  529 us
    all_to_all x1, waiting for transfers between devices, per_device(): lax.all_to_all(summed, 'expert', split_axis=0, concat_axis=0, tiled=True)  276 us
    all_to_all x1, blocking collectives, per_device(): lax.all_to_all(sectioned, 'expert', split_axis=0, concat_axis=0, tiled=True)  191 us
    ppermute x3, waiting for transfers between devices, from_behind(): return lax.ppermute(block, axis, route)  103 us
    all_to_all x1, blocking collectives, per_device(): lax.all_to_all(sectioned_fresh, 'expert', split_axis=0, concat_axis=0, ti...  45.4 us
    all_to_all x1, blocking collectives, per_device(): lax.all_to_all(chosen, 'expert', split_axis=0, concat_axis=0, tiled=True)  35.7 us
  transfers between devices with their start and end apart: 5, of which 3 were waited for; matrix products, arithmetic and copies ran while one was open for 1% of the time, Pallas kernels for 0%

profile of v1, /device:TPU:25, one launch (start us, length us, event | category | flops | bytes accessed | tf_op | source)
XLA Modules:
  0.0 1278.4 jit_solution(2905322084862689778)
XLA Ops:
  7.2 0.0 copy-start
  8.5 0.0 copy-done
  8.5 4.3 fusion
  12.8 6.3 copy.44
  19.1 7.6 reshape.58
  26.7 0.0 copy-start.6
  26.7 190.7 %all_to_all.20 = bf16[64,12,4,640]{3,2,1,0:T(4,128)(2,1)S(1)} all-to-all(bf16[64,12,4,640]{3,2,1,0:T(4,128)(2,1)} %reshape.58), channel_id=1, replica_groups=mesh['dp'=8,'expert'=64] {'expert'}, dimensions={0} | all-to-all | bytes 7864320 | tf_op jit(solution)/shard_map/all_to_all | solution.py:67
  217.4 0.0 copy-done.6
  217.4 0.7 fusion.1
  218.1 2.7 copy.46
  220.8 0.0 copy-start.2
  220.8 8.7 all-to-all-start.1
  229.5 0.0 all-gather.3.cloned.1.call-start
  229.6 0.0 copy-done.2
  229.6 1.3 fusion.8
  230.9 3.2 constant_dynamic-slice_fusion.3
  234.1 2.9 copy.41
  237.0 4.2 collective-permute-start
  241.2 2.9 copy.42
  244.1 7.2 collective-permute-start.1
  251.3 2.9 copy.43
  254.1 5.3 collective-permute-start.2
  259.4 2.8 copy.40
  262.2 275.9 %all-to-all-done.1 = f32[64,12,640]{2,1,0:T(8,128)S(1)} async-done(((f32[64,12,640]{2,1,0:T(8,128)}), f32[64,12,640]{2,1,0:T(8,128)S(1)}, u32[]{:S(2)}, u32[]{:S(2)}) %all-to-all-start.1) | async-done | bytes 1966112 | tf_op jit(solution)/shard_map/all_to_all | solution.py:70
  538.1 1.4 reshape.60
  539.5 0.0 collective-permute-done
  539.5 103.2 %collective-permute-done.1 = f32[768,640]{1,0:T(8,128)} collective-permute-done((f32[768,640]{1,0:T(8,128)}, f32[768,640]{1,0:T(8,128)}, u32[]{:S(2)}, u32[]{:S(2)}) %collective-permute-start.1) | collective-permute-done | bytes 1966112 | tf_op jit(solution)/shard_map/ppermute | solution.py:18
  642.7 0.0 collective-permute-done.2
  642.7 5.6 fusion.5
  648.3 0.0 all-gather.3.cloned.1.call-update
  648.3 529.0 %all-gather.3.cloned.1.call-done = f32[6144,640]{1,0:T(8,128)} async-done(((f32[768,640]{1,0:T(8,128)}), f32[6144,640]{1,0:T(8,128)}) %all-gather.3.cloned.1.call-update) | async-done | bytes 15728656 | tf_op jit(solution)/shard_map/all_gather | solution.py:74
  1177.3 0.0 copy-start.3
  1177.3 0.0 copy-start.4
  1177.3 0.0 copy-start.5
  1177.3 6.6 reduce_sum.9
  1184.0 0.0 copy-done.3
  1184.0 0.0 copy-done.4
  1184.0 0.0 copy-done.5
  1184.0 1.0 fusion.27
  1185.0 0.2 reshape.67
  1185.2 0.5 broadcast.46
  1185.7 1.4 reduce
  1187.1 0.2 reshape.69
  1187.3 45.4 %all_to_all.21 = bf16[64,2,480]{2,1,0:T(2,128)(2,1)S(1)} all-to-all(bf16[64,2,480]{2,1,0:T(2,128)(2,1)S(1)} %reshape.69), channel_id=1, replica_groups=mesh['dp'=8,'expert'=64] {'expert'}, dimensions={0} | all-to-all | bytes 245760 | tf_op jit(solution)/shard_map/all_to_all | solution.py:82
  1232.7 0.2 reshape.70
  1232.9 0.3 fusion.6
  1233.3 0.4 copy.48
  1233.7 35.7 %all_to_all.22 = bf16[64,1,4,960]{3,2,1,0:T(4,128)(2,1)S(1)} all-to-all(bf16[64,1,4,960]{3,2,1,0:T(4,128)(2,1)S(1)} %copy.48), channel_id=1, replica_groups=mesh['dp'=8,'expert'=64] {'expert'}, dimensions={0} | all-to-all | bytes 983040 | tf_op jit(solution)/shard_map/all_to_all | solution.py:87
  1269.4 0.0 copy-start.1
  1269.4 0.2 copy.49
  1269.5 0.8 reshape.63
  1270.3 0.3 copy.50
  1270.6 1.0 broadcast_in_dim_reshape.3
  1271.5 0.0 copy-done.1
  (2 shorter events, 0.1 us)
Async XLA Ops:
  7.2 1.4 copy-start
  26.7 190.7 %copy-start.6 = (s32[64]{0:T(128)S(1)}, s32[64]{0:T(128)}, u32[]{:S(2)}) copy-start(s32[64]{0:T(128)} %param.12) | copy-start | bytes 772
  220.8 8.8 copy-start.2
  220.8 317.3 %all-to-all-start.1 = ((f32[64,12,640]{2,1,0:T(8,128)}), f32[64,12,640]{2,1,0:T(8,128)S(1)}, u32[]{:S(2)}, u32[]{:S(2)}) async-start(f32[64,12,640]{2,1,0:T(8,128)} %copy.46), calls=%async_computation.1 | async-start | bytes 5242880 | tf_op jit(solution)/shard_map/all_to_all | solution.py:70
  229.5 947.9 %all-gather.3.cloned.1.call-start = ((), (), s32[]{:S(2)}) async-start(), calls=%async_computation.4 | async-start | bytes 17694720 | tf_op jit(solution)/shard_map/all_gather | solution.py:74
  237.0 302.5 %collective-permute-start = (f32[768,640]{1,0:T(8,128)}, f32[768,640]{1,0:T(8,128)}, u32[]{:S(2)}, u32[]{:S(2)}) collective-permute-start(f32[768,640]{1,0:T(8,128)} %bitcast.77), channel_id=1, source_target_pairs={{48,0},{49,1},{50,2},{51,3},{52,4},{53,5},{54,6},{55,7},{56,8},{57... | collective-permute-start | bytes 5898248 | tf_op jit(solution)/shard_map/ppermute | solution.py:18
  244.1 398.7 %collective-permute-start.1 = (f32[768,640]{1,0:T(8,128)}, f32[768,640]{1,0:T(8,128)}, u32[]{:S(2)}, u32[]{:S(2)}) collective-permute-start(f32[768,640]{1,0:T(8,128)} %bitcast.78), channel_id=1, source_target_pairs={{32,0},{33,1},{34,2},{35,3},{36,4},{37,5},{38,6},{39,7},{40,8},{41... | collective-permute-start | bytes 5898248 | tf_op jit(solution)/shard_map/ppermute | solution.py:18
  254.1 388.6 %collective-permute-start.2 = (f32[768,640]{1,0:T(8,128)}, f32[768,640]{1,0:T(8,128)}, u32[]{:S(2)}, u32[]{:S(2)}) collective-permute-start(f32[768,640]{1,0:T(8,128)} %bitcast.79), channel_id=1, source_target_pairs={{16,0},{17,1},{18,2},{19,3},{20,4},{21,5},{22,6},{23,7},{24,8},{25... | collective-permute-start | bytes 5898248 | tf_op jit(solution)/shard_map/ppermute | solution.py:18
  1177.3 6.6 copy-start.3
  1177.3 6.6 copy-start.4
  1177.3 6.7 copy-start.5
  1269.4 2.2 copy-start.1
Sparse Core Ops, SparseCore 0:
  648.5 528.8 all-gather.2
